TPU v7x, 256 devices: a whole 4x4x8 slice. The times are simulated.
256 devices in a mesh: gx: 8 (over x, core), gy: 32 (over y, z).
Axes of the slice: x: 4, y: 4, z: 8, core: 2. Of those that a mesh axis runs over, the one named last changes fastest.
Arguments:
- features: float32 [64, 524288], P(None, ('gx', 'gy')), may hold values from -6 to 6
- cotangent: float32 [64, 524288], P(None, ('gx', 'gy')), may hold values from -6 to 6
- edge_src: int32 [8, 524288], P(None, ('gx', 'gy')), may hold values from 0 to 2559
- send_rows: int32 [4, 32768], P(None, ('gx', 'gy')), may hold values from 0 to 2047
- fine_to_coarse: int32 [524288], P(('gx', 'gy')), may hold values from 0 to 2047
- coarse_to_fine: int32 [524288], P(('gx', 'gy')), may hold values from 0 to 2047
- coarse_edges: int32 [2, 8192], replicated, may hold values from 0 to 2047
- edge_in: float32 [64, 128], replicated, may hold values from -0.5 to 0.5
- edge_out: float32 [64, 64], replicated, may hold values from -0.75 to 0.75
- node_in: float32 [64, 128], replicated, may hold values from -0.5 to 0.5
- node_out: float32 [64, 64], replicated, may hold values from -0.75 to 0.75
- coarse_in: float32 [64, 64], replicated, may hold values from -0.75 to 0.75
- coarse_out: float32 [64, 64], replicated, may hold values from -0.75 to 0.75
- coarse_mix: float32 [64, 64], replicated, may hold values from -0.75 to 0.75
- up_in: float32 [64, 128], replicated, may hold values from -0.5 to 0.5
- up_out: float32 [64, 64], replicated, may hold values from -0.75 to 0.75
- biases: float32 [4, 64], replicated, may hold values from -3 to 3
Outputs:
- output: float32 [64, 524288], P(None, ('gx', 'gy'))
- grad_features: float32 [64, 524288], P(None, ('gx', 'gy'))
- grad_edge_in: float32 [64, 128], replicated
- grad_edge_out: float32 [64, 64], replicated
- grad_node_in: float32 [64, 128], replicated
- grad_node_out: float32 [64, 64], replicated
- grad_coarse_in: float32 [64, 64], replicated
- grad_coarse_out: float32 [64, 64], replicated
- grad_coarse_mix: float32 [64, 64], replicated
- grad_up_in: float32 [64, 128], replicated
- grad_up_out: float32 [64, 64], replicated
- grad_biases: float32 [4, 64], replicated
Inputs may be any that keep to these rules, and one draw needn't show every extreme that they name: `edge_src`: indexes the receiver partition's 2048 own nodes, then the four received packets in the order of the first step. `send_rows`: partition-local node numbers.
All inputs are finite; a program needn't handle non-finite values.
Results may differ from a plain program's by a relative error of at most 0.0003.
Values sent between devices are 32-bit elements; how exact they have to be, the bound alone decides.
A program may use at most 64 MiB of HBM per device.

v0:
```python
from functools import partial
import math
import jax
import jax.numpy as jnp
from jax import lax
from jax.sharding import PartitionSpec as P

COARSE = 2048


def passed_along(value, axis, steps):
    count = lax.axis_size(axis)
    leading, last = (max(0, -steps), min(count, count - steps))
    return lax.ppermute(value, axis, [(source, source + steps) for source in range(leading, last)])


def matmul(left_side, right_side):
    return jnp.dot(
        left_side, right_side, precision=lax.Precision.HIGHEST, preferred_element_type=jnp.float32
    )


def swish(values):
    return values * jax.nn.sigmoid(values)


def fine_update(
    latent, extended, edge_in, edge_out, node_in, node_out, edge_bias, node_bias, sources
):
    feature_count = latent.shape[0]
    receiver_part = matmul(edge_in[:, :feature_count], latent)
    sender_part = matmul(edge_in[:, feature_count:], extended)
    hidden = swish(receiver_part[:, None, :] + sender_part[:, sources] + edge_bias[:, None, None])
    summed = matmul(edge_out, jnp.sum(hidden, axis=1))
    activation = swish(
        matmul(node_in[:, :feature_count], latent)
        + matmul(node_in[:, feature_count:], summed)
        + node_bias[:, None]
    )
    return latent + matmul(node_out, activation)


def coarse_node(pooled, coarse_in, coarse_out, coarse_bias):
    return pooled + matmul(coarse_out, swish(matmul(coarse_in, pooled) + coarse_bias[:, None]))


def coarse_edge(nodes, coarse_mix, coarse_edges):
    gathered = nodes[:, coarse_edges[0]]
    summed = jnp.zeros_like(nodes).at[:, coarse_edges[1]].add(gathered)
    factor = (nodes.shape[1] / coarse_edges.shape[1]) ** 0.5
    return nodes + matmul(coarse_mix, summed) * factor


def up_update(middle, looked, up_in, up_out, up_bias):
    feature_count = middle.shape[0]
    activation = swish(
        matmul(up_in[:, :feature_count], middle)
        + matmul(up_in[:, feature_count:], looked)
        + up_bias[:, None]
    )
    return middle + matmul(up_out, activation)


def block_width(node_count):
    return math.gcd(node_count, 1024)


def one_hot_block(index_block, table_width):
    return (index_block[:, None] == jnp.arange(table_width, dtype=jnp.int32)[None, :]).astype(
        jnp.float32
    )


def pool_nodes(values, index, table_width):
    feature_count, node_count = values.shape
    width = block_width(node_count)
    blocks = node_count // width
    value_blocks = values.reshape(feature_count, blocks, width).transpose(1, 0, 2)
    index_blocks = index.reshape(blocks, width)

    def add_block(total, items):
        return (total + matmul(items[0], one_hot_block(items[1], table_width)), None)

    start = jnp.zeros((feature_count, table_width), jnp.float32)
    total, unused = lax.scan(add_block, start, (value_blocks, index_blocks))
    return total


def look_nodes(table, index):
    feature_count, table_width = table.shape
    node_count = index.shape[0]
    width = block_width(node_count)
    blocks = node_count // width
    index_blocks = index.reshape(blocks, width)

    def read_block(index_block):
        selector = one_hot_block(index_block, table_width)
        return lax.dot_general(
            table,
            selector,
            (((1,), (1,)), ((), ())),
            precision=lax.Precision.HIGHEST,
            preferred_element_type=jnp.float32,
        )

    result = lax.map(read_block, index_blocks)
    return result.transpose(1, 0, 2).reshape(feature_count, node_count)


def pass_rows(packet, offset):
    return passed_along(packet, "gx", offset)


def pass_cols(packet, offset):
    return passed_along(packet, "gy", offset)


def coarse_total(table):
    return lax.psum(table, ("gx", "gy"))


def local(
    features,
    cotangent,
    edge_src,
    send_rows,
    fine_to_coarse,
    coarse_to_fine,
    coarse_edges,
    edge_in,
    edge_out,
    node_in,
    node_out,
    coarse_in,
    coarse_out,
    coarse_mix,
    up_in,
    up_out,
    biases,
):
    local_nodes = features.shape[1]
    halo_rows = send_rows.shape[1]
    pool_scale = (COARSE / (local_nodes * lax.axis_size("gx") * lax.axis_size("gy"))) ** 0.5
    packets = features[:, send_rows]
    extended = jnp.concatenate(
        [
            features,
            pass_rows(packets[:, 0], 1),
            pass_rows(packets[:, 1], -1),
            pass_cols(packets[:, 2], 1),
            pass_cols(packets[:, 3], -1),
        ],
        axis=1,
    )
    middle, fine_back = jax.vjp(
        partial(fine_update, sources=edge_src),
        features,
        extended,
        edge_in,
        edge_out,
        node_in,
        node_out,
        biases[0],
        biases[1],
    )
    pooled_part = pool_nodes(middle, fine_to_coarse, COARSE) * pool_scale
    pooled = coarse_total(pooled_part)
    nodes, node_back = jax.vjp(coarse_node, pooled, coarse_in, coarse_out, biases[2])
    mixed, mix_back = jax.vjp(partial(coarse_edge, coarse_edges=coarse_edges), nodes, coarse_mix)
    looked = look_nodes(mixed, coarse_to_fine)
    output, up_back = jax.vjp(up_update, middle, looked, up_in, up_out, biases[3])
    grad_middle, grad_looked, grad_up_in, grad_up_out, grad_up_bias = up_back(cotangent)
    grad_mixed_part = pool_nodes(grad_looked, coarse_to_fine, COARSE)
    grad_nodes_part, grad_mix = mix_back(grad_mixed_part)
    grad_nodes = coarse_total(grad_nodes_part)
    grad_pooled, grad_coarse_in, grad_coarse_out, grad_coarse_bias = node_back(grad_nodes)
    grad_middle = grad_middle + look_nodes(grad_pooled, fine_to_coarse) * pool_scale
    (
        grad_own,
        grad_ext,
        grad_edge_in,
        grad_edge_out,
        grad_node_in,
        grad_node_out,
        grad_edge_bias,
        grad_node_bias,
    ) = fine_back(grad_middle)
    pieces = [
        grad_ext[:, local_nodes + slot * halo_rows : local_nodes + (slot + 1) * halo_rows]
        for slot in range(4)
    ]
    returned = jnp.stack(
        [
            pass_rows(pieces[0], -1),
            pass_rows(pieces[1], 1),
            pass_cols(pieces[2], -1),
            pass_cols(pieces[3], 1),
        ],
        axis=1,
    )
    grad_features = (
        grad_own
        + grad_ext[:, :local_nodes]
        + jnp.zeros_like(features).at[:, send_rows].add(returned)
    )
    fine_biases = jnp.stack([grad_edge_bias, grad_node_bias, grad_up_bias])
    summed = lax.psum(
        (
            grad_edge_in,
            grad_edge_out,
            grad_node_in,
            grad_node_out,
            grad_mix,
            grad_up_in,
            grad_up_out,
            fine_biases,
        ),
        ("gx", "gy"),
    )
    grad_biases = jnp.stack([summed[7][0], summed[7][1], grad_coarse_bias, summed[7][2]])
    return (
        output,
        grad_features,
        summed[0],
        summed[1],
        summed[2],
        summed[3],
        grad_coarse_in,
        grad_coarse_out,
        summed[4],
        summed[5],
        summed[6],
        grad_biases,
    )


def solution(mesh):
    in_specs = (
        P(None, ("gx", "gy")),
        P(None, ("gx", "gy")),
        P(None, ("gx", "gy")),
        P(None, ("gx", "gy")),
        P(("gx", "gy")),
        P(("gx", "gy")),
        P(),
        P(),
        P(),
        P(),
        P(),
        P(),
        P(),
        P(),
        P(),
        P(),
        P(),
    )
    out_specs = (
        P(None, ("gx", "gy")),
        P(None, ("gx", "gy")),
        P(),
        P(),
        P(),
        P(),
        P(),
        P(),
        P(),
        P(),
        P(),
        P(),
    )
    return jax.shard_map(local, mesh=mesh, in_specs=in_specs, out_specs=out_specs, check_vma=False)
```

profile of v0, /device:TPU:4, one launch (start us, length us, event | category | flops | bytes accessed | tf_op | source)
XLA Modules:
  0.0 1284.9 jit_solution(6008554091809120378)
XLA Ops:
  11.8 4.5 collective-permute-start.2
  35.8 54.7 %gather_fusion.1 = f32[16384,64]{1,0:T(8,128)} fusion(f32[64,2560]{0,1:T(8,128)S(1)} %copy.65, s32[16384]{0:T(1024)S(1)} %broadcast_clamp_fusion), kind=kCustom, calls=%fused_computation.1 | custom fusion | bytes 8454144 | tf_op jit(solution)/shard_map/jvp()/gather | solution.py:33
  90.6 4.8 multiply_reduce_fusion
  100.4 7.0 while.44
  100.5 3.5 fusion.178
  104.0 3.5 fusion.178
  110.1 254.7 %all-reduce.11.cloned.1.call-done = f32[64,2048]{1,0:T(8,128)} async-done(((f32[64,2048]{1,0:T(8,128)}), f32[64,2048]{1,0:T(8,128)}) %all-reduce.11.cloned.1.call-update) | async-done | bytes 524304 | tf_op jit(solution)/shard_map/psum | solution.py:119
  370.4 90.5 %scatter_custom_fusion = f32[64,2048]{0,1:T(8,128)S(1)} fusion(s32[8192]{0:T(1024)} %bitcast.245, f32[64,2048]{0,1:T(8,128)} %copy.67, s32[8192]{0:T(1024)} %broadcast_clamp_fusion.2, f32[]{:T(128)} %constant.19.clone.1), kind=kCustom, calls=%fused_computation.44 | custom fusion | flops 524288 | bytes 524800 | tf_op jit(solution)/shard_map/jvp()/scatter-add | solution.py:49
  463.0 11.0 while.42
  463.1 5.5 fusion.174
  468.6 5.5 fusion.174
  485.0 10.4 while.45
  485.0 5.1 fusion.180
  490.1 5.3 fusion.180
  502.6 103.6 %scatter_custom_fusion.1 = f32[64,2048]{0,1:T(8,128)} fusion(f32[64,2048]{0,1:T(8,128)} %copy.71, s32[8192]{0:T(1024)} %bitcast.243, f32[]{:T(128)} %constant.19.clone.1, pred[8192]{0:T(1024)(128)(4,1)S(1)} %compare_and_fusion, f32[64,2048]{0,1:T(8,128)} %copy.70, s32[8192]{0:T(1024)S(1)} %broadcast_clamp_fusion.1), kind=kCustom, calls=%fused_computation.42 | custom fusion | flops 1048576 | bytes 1614336 | tf_op jit(solution)/shard_map/transpose(jvp())/scatter-add | solution.py:48
  611.0 248.5 %all-reduce.13.cloned.1.call-done = f32[64,2048]{1,0:T(8,128)} async-done(((f32[64,2048]{1,0:T(8,128)}), f32[64,2048]{1,0:T(8,128)}) %all-reduce.13.cloned.1.call-update) | async-done | bytes 524304 | tf_op jit(solution)/shard_map/psum | solution.py:119
  864.6 8.9 while.43
  864.6 4.4 fusion.176
  869.1 4.4 fusion.176
  889.0 5.7 fusion.21
  894.7 3.2 copy-done.1
  905.0 88.0 %scatter_custom_fusion.2 = f32[64,2560]{0,1:T(8,128)S(1)} fusion(s32[16384]{0:T(1024)S(1)} %bitcast.240, f32[16384,64]{1,0:T(8,128)} %bitcast.227, f32[]{:T(128)} %constant.19.clone.1), kind=kCustom, calls=%fused_computation.85 | custom fusion | flops 1048576 | bytes 655872 | tf_op jit(solution)/shard_map/transpose(jvp())/scatter-add | solution.py:33
  1015.1 3.7 scatter_fusion
  1019.9 246.4 %all-reduce.15.cloned.1.call-done = (f32[64,128]{1,0:T(8,128)}, f32[64,64]{1,0:T(8,128)}, f32[64,128]{1,0:T(8,128)}, f32[64,64]{1,0:T(8,128)}, f32[64,64]{1,0:T(...) async-done(((f32[64,128]{1,0:T(8,128)}, f32[64,64]{1,0:T(8,128)}, f32[64,128]{1,0:T(8,128)}, f32[64,64]{1,0:T(8,128)}, f32[64,64]{1,0:T(8,128)}, ...) | async-done | bytes 164624 | tf_op jit(solution)/shard_map/psum | solution.py:207
  (183 shorter events, 124.3 us)
Async XLA Ops:
  7.2 360.1 %copy-start = (f32[64,64]{1,0:T(8,128)S(1)}, f32[64,64]{1,0:T(8,128)}, u32[]{:S(2)}) copy-start(f32[64,64]{1,0:T(8,128)} %param.37) | copy-start | bytes 49156
  7.2 357.6 %all-reduce.11.cloned.1.call-start = ((), (), s32[]{:S(2)}) async-start(), calls=%async_computation | async-start | bytes 1048576 | tf_op jit(solution)/shard_map/psum | solution.py:119
  10.5 22.6 %collective-permute-start.3 = (f32[64,128]{1,0:T(8,128)S(1)}, f32[64,128]{1,0:T(8,128)S(1)}, u32[]{:S(2)}, u32[]{:S(2)}) collective-permute-start(f32[64,128]{1,0:T(8,128)S(1)} %get-tuple-element.218), channel_id=1, source_target_pairs={{1,0},{2,1},{3,2},{4,3},{5,4},{6,5},{7,6},{8,7},{9,8},{10,9},{11,1... | collective-permute-start | bytes 98312 | tf_op jit(solution)/shard_map/ppermute | solution.py:14
  11.8 21.3 %collective-permute-start.2 = (f32[64,128]{1,0:T(8,128)S(1)}, f32[64,128]{1,0:T(8,128)S(1)}, u32[]{:S(2)}, u32[]{:S(2)}) collective-permute-start(f32[64,128]{1,0:T(8,128)S(1)} %get-tuple-element.219), channel_id=1, source_target_pairs={{0,1},{1,2},{2,3},{3,4},{4,5},{5,6},{6,7},{7,8},{8,9},{9,10},{10,1... | collective-permute-start | bytes 98312 | tf_op jit(solution)/shard_map/ppermute | solution.py:14
  16.3 16.7 %collective-permute-start.1 = (f32[64,128]{1,0:T(8,128)S(1)}, f32[64,128]{1,0:T(8,128)S(1)}, u32[]{:S(2)}, u32[]{:S(2)}) collective-permute-start(f32[64,128]{1,0:T(8,128)S(1)} %get-tuple-element.220), channel_id=1, source_target_pairs={{32,0},{64,32},{96,64},{128,96},{160,128},{192,160},{224,192},{33,... | collective-permute-start | bytes 98312 | tf_op jit(solution)/shard_map/ppermute | solution.py:14
  18.3 14.7 %collective-permute-start = (f32[64,128]{1,0:T(8,128)S(1)}, f32[64,128]{1,0:T(8,128)S(1)}, u32[]{:S(2)}, u32[]{:S(2)}) collective-permute-start(f32[64,128]{1,0:T(8,128)S(1)} %get-tuple-element.221), channel_id=1, source_target_pairs={{0,32},{32,64},{64,96},{96,128},{128,160},{160,192},{192,224},{1,3... | collective-permute-start | bytes 98312 | tf_op jit(solution)/shard_map/ppermute | solution.py:14
  23.7 12.2 copy-start.23
  27.2 63.4 %copy-start.3 = (f32[64,2048]{0,1:T(8,128)}, f32[64,2048]{0,1:T(8,128)S(1)}, u32[]{:S(2)}) copy-start(f32[64,2048]{0,1:T(8,128)S(1)} %fusion.81) | copy-start | bytes 1572868
  90.6 9.0 copy-start.29
  90.6 9.8 copy-start.16
  100.4 264.3 %copy-start.21 = (f32[64,64]{1,0:T(8,128)S(1)}, f32[64,64]{1,0:T(8,128)}, u32[]{:S(2)}) copy-start(f32[64,64]{1,0:T(8,128)} %param.36) | copy-start | bytes 49156
  107.4 353.4 %copy-start.20 = (f32[64,64]{1,0:T(8,128)S(1)}, f32[64,64]{1,0:T(8,128)}, u32[]{:S(2)}) copy-start(f32[64,64]{1,0:T(8,128)} %param.38) | copy-start | bytes 49156
  108.3 751.2 %all-reduce.13.cloned.1.call-start = ((), (), s32[]{:S(2)}) async-start(), calls=%async_computation.1 | async-start | bytes 1048576 | tf_op jit(solution)/shard_map/psum | solution.py:119
  463.0 11.1 copy-start.28
  463.0 15.5 %copy-start.25 = (f32[64,64]{1,0:T(8,128)S(1)}, f32[64,64]{1,0:T(8,128)}, u32[]{:S(2)}) copy-start(f32[64,64]{1,0:T(8,128)} %param.40) | copy-start | bytes 49156
  608.5 657.8 %all-reduce.15.cloned.1.call-start = ((), (), s32[]{:S(2)}) async-start(), calls=%async_computation.2 | async-start | bytes 462848 | tf_op jit(solution)/shard_map/psum | solution.py:207
  864.6 15.3 %copy-start.30 = (f32[64,64]{1,0:T(8,128)S(1)}, f32[64,64]{1,0:T(8,128)}, u32[]{:S(2)}) copy-start(f32[64,64]{1,0:T(8,128)} %param.35) | copy-start | bytes 49156
  874.3 14.6 %copy-start.4 = (f32[64,2048]{0,1:T(8,128)S(1)}, f32[64,2048]{0,1:T(8,128)}, u32[]{:S(2)}) copy-start(f32[64,2048]{0,1:T(8,128)} %copy-done.3) | copy-start | bytes 1572868
  897.9 95.0 %copy-start.6 = (f32[64,2560]{1,0:T(8,128)S(1)}, f32[64,2560]{1,0:T(8,128)}, u32[]{:S(2)}) copy-start(f32[64,2560]{1,0:T(8,128)} %copy-done.5) | copy-start | bytes 1966084
  992.9 276.1 %copy-start.27 = (f32[64]{0:T(128)S(1)}, f32[64]{0:T(128)}, u32[]{:S(2)}) copy-start(f32[64]{0:T(128)} %get-tuple-element.231) | copy-start | bytes 772
  998.7 16.2 %collective-permute-start.4 = (f32[64,128]{1,0:T(8,128)S(1)}, f32[64,128]{1,0:T(8,128)S(1)}, u32[]{:S(2)}, u32[]{:S(2)}) collective-permute-start(f32[64,128]{1,0:T(8,128)S(1)} %get-tuple-element.214), channel_id=1, source_target_pairs={{32,0},{64,32},{96,64},{128,96},{160,128},{192,160},{224,192},{33,... | collective-permute-start | bytes 98312 | tf_op jit(solution)/shard_map/ppermute | solution.py:14
  1000.6 14.3 %collective-permute-start.7 = (f32[64,128]{1,0:T(8,128)S(1)}, f32[64,128]{1,0:T(8,128)S(1)}, u32[]{:S(2)}, u32[]{:S(2)}) collective-permute-start(f32[64,128]{1,0:T(8,128)S(1)} %get-tuple-element.215), channel_id=1, source_target_pairs={{0,1},{1,2},{2,3},{3,4},{4,5},{5,6},{6,7},{7,8},{8,9},{9,10},{10,1... | collective-permute-start | bytes 98312 | tf_op jit(solution)/shard_map/ppermute | solution.py:14
  1002.5 12.3 collective-permute-start.6
  1003.8 11.1 collective-permute-start.5
  (18 other events, 85.2 us)
Sparse Core Ops, SparseCore 0:
  108.4 256.2 all-reduce.10
  608.6 250.7 all-reduce.12
  1009.7 256.5 all-reduce.14
where the time goes:
time: 1300 us; the launch traced here: 1280 us
  waiting for transfers between devices  750 us (58%)
  other arithmetic  308 us (24%)
  matrix products  101 us (8%)
  local copies, waits for them, and re-layouts  93.4 us (7%)
  starting transfers between devices  17.9 us (1%)
  between operations  15 us (1%)
    psum x2, waiting for transfers between devices, coarse_total(): return lax.psum(table, ('gx', 'gy'))  503 us
    psum x1, waiting for transfers between devices, local(): lax.psum((grad_edge_in, grad_edge_out, grad_node_in, grad_node_out, grad_...  246 us
    scatter-add x1, other arithmetic, coarse_edge(): gathered = nodes[:, coarse_edges[0]]  104 us
    scatter-add x1, other arithmetic, coarse_edge(): summed = jnp.zeros_like(nodes).at[:, coarse_edges[1]].add(gathered)  90.5 us
    scatter-add x1, other arithmetic, fine_update(): sender_part[:, sources]  88 us
    dot_general x40, matrix products, matmul(): jnp.dot(left_side, right_side, precision=lax.Precision.HIGHEST, preferred...  80.9 us
    gather x1, local copies, waits for them, and re-layouts, fine_update(): sender_part[:, sources]  54.7 us
  transfers between devices with their start and end apart: 11, of which 3 were waited for; matrix products, arithmetic and copies ran while one was open for 2% of the time, Pallas kernels for 0%

commit v1 on v0

--- a/solution.py
+++ b/solution.py
@@ -205,17 +205,20 @@
     )
     fine_biases = jnp.stack([grad_edge_bias, grad_node_bias, grad_up_bias])
     summed = lax.psum(
-        (
-            grad_edge_in,
-            grad_edge_out,
-            grad_node_in,
-            grad_node_out,
-            grad_mix,
-            grad_up_in,
-            grad_up_out,
-            fine_biases,
+        lax.psum(
+            (
+                grad_edge_in,
+                grad_edge_out,
+                grad_node_in,
+                grad_node_out,
+                grad_mix,
+                grad_up_in,
+                grad_up_out,
+                fine_biases,
+            ),
+            "gy",
         ),
-        ("gx", "gy"),
+        "gx",
     )
     grad_biases = jnp.stack([summed[7][0], summed[7][1], grad_coarse_bias, summed[7][2]])
     return (

time: 1300 us -> 1250 us (0.962)
  waiting for transfers between devices: 750 us -> 701 us
    psum x1, waiting for transfers between devices: 246 us -> 143 us  [local(): lax.psum((grad_edge_in, grad_edge_out, grad_node_in, grad_node_out, grad_...]
    psum x0 -> x1, waiting for transfers between devices: none -> 56.1 us  [local(): lax.psum(lax.psum((grad_edge_in, grad_edge_out, grad_node_in, grad_node_o...]
  transfers between devices with their start and end apart: 11 -> 12, of which waited for: 3 -> 4; matrix products, arithmetic and copies ran while one was open for 2% -> 2% of each run, Pallas kernels for 0% -> 0%
where the time goes in v1:
time: 1250 us; the launch traced here: 1240 us
  waiting for transfers between devices  701 us (56%)
  other arithmetic  308 us (25%)
  matrix products  99.8 us (8%)
  local copies, waits for them, and re-layouts  93.5 us (7%)
  starting transfers between devices  17.9 us (1%)
  between operations  15 us (1%)
    psum x2, waiting for transfers between devices, coarse_total(): return lax.psum(table, ('gx', 'gy'))  503 us
    psum x1, waiting for transfers between devices, local(): lax.psum((grad_edge_in, grad_edge_out, grad_node_in, grad_node_out, grad_...  143 us
    scatter-add x1, other arithmetic, coarse_edge(): gathered = nodes[:, coarse_edges[0]]  104 us
    scatter-add x1, other arithmetic, coarse_edge(): summed = jnp.zeros_like(nodes).at[:, coarse_edges[1]].add(gathered)  90.4 us
    scatter-add x1, other arithmetic, fine_update(): sender_part[:, sources]  88 us
    dot_general x40, matrix products, matmul(): jnp.dot(left_side, right_side, precision=lax.Precision.HIGHEST, preferred...  80 us
    psum x1, waiting for transfers between devices, local(): lax.psum(lax.psum((grad_edge_in, grad_edge_out, grad_node_in, grad_node_o...  56.1 us
    gather x1, local copies, waits for them, and re-layouts, fine_update(): sender_part[:, sources]  54.8 us
  transfers between devices with their start and end apart: 12, of which 4 were waited for; matrix products, arithmetic and copies ran while one was open for 2% of the time, Pallas kernels for 0%

profile of v1, /device:TPU:4, one launch (start us, length us, event | category | flops | bytes accessed | tf_op | source)
XLA Modules:
  0.0 1235.9 jit_solution(3382150932103333819)
XLA Ops:
  11.8 4.5 collective-permute-start.2
  35.8 54.8 %gather_fusion.1 = f32[16384,64]{1,0:T(8,128)} fusion(f32[64,2560]{0,1:T(8,128)S(1)} %copy.65, s32[16384]{0:T(1024)S(1)} %broadcast_clamp_fusion), kind=kCustom, calls=%fused_computation.1 | custom fusion | bytes 8454144 | tf_op jit(solution)/shard_map/jvp()/gather | solution.py:33
  90.6 4.8 multiply_reduce_fusion
  100.5 7.0 while.44
  100.5 3.5 fusion.178
  104.0 3.5 fusion.178
  110.1 254.5 %all-reduce.13.cloned.1.call-done = f32[64,2048]{1,0:T(8,128)} async-done(((f32[64,2048]{1,0:T(8,128)}), f32[64,2048]{1,0:T(8,128)}) %all-reduce.13.cloned.1.call-update) | async-done | bytes 524304 | tf_op jit(solution)/shard_map/psum | solution.py:119
  370.3 90.4 %scatter_custom_fusion = f32[64,2048]{0,1:T(8,128)S(1)} fusion(s32[8192]{0:T(1024)} %bitcast.245, f32[64,2048]{0,1:T(8,128)} %copy.67, s32[8192]{0:T(1024)} %broadcast_clamp_fusion.2, f32[]{:T(128)} %constant.19.clone.1), kind=kCustom, calls=%fused_computation.44 | custom fusion | flops 524288 | bytes 524800 | tf_op jit(solution)/shard_map/jvp()/scatter-add | solution.py:49
  462.9 11.0 while.42
  462.9 5.5 fusion.174
  468.4 5.5 fusion.174
  484.9 10.3 while.45
  484.9 5.1 fusion.180
  490.0 5.2 fusion.180
  502.4 103.6 %scatter_custom_fusion.1 = f32[64,2048]{0,1:T(8,128)} fusion(f32[64,2048]{0,1:T(8,128)} %copy.71, s32[8192]{0:T(1024)} %bitcast.243, f32[]{:T(128)} %constant.19.clone.1, pred[8192]{0:T(1024)(128)(4,1)S(1)} %compare_and_fusion, f32[64,2048]{0,1:T(8,128)} %copy.70, s32[8192]{0:T(1024)S(1)} %broadcast_clamp_fusion.1), kind=kCustom, calls=%fused_computation.42 | custom fusion | flops 1048576 | bytes 1614336 | tf_op jit(solution)/shard_map/transpose(jvp())/scatter-add | solution.py:48
  610.8 248.3 %all-reduce.15.cloned.1.call-done = f32[64,2048]{1,0:T(8,128)} async-done(((f32[64,2048]{1,0:T(8,128)}), f32[64,2048]{1,0:T(8,128)}) %all-reduce.15.cloned.1.call-update) | async-done | bytes 524304 | tf_op jit(solution)/shard_map/psum | solution.py:119
  864.4 8.9 while.43
  864.4 4.4 fusion.176
  868.8 4.4 fusion.176
  888.7 5.7 fusion.21
  903.9 88.0 %scatter_custom_fusion.2 = f32[64,2560]{0,1:T(8,128)S(1)} fusion(s32[16384]{0:T(1024)S(1)} %bitcast.240, f32[16384,64]{1,0:T(8,128)} %bitcast.227, f32[]{:T(128)} %constant.19.clone.1), kind=kCustom, calls=%fused_computation.85 | custom fusion | flops 1048576 | bytes 655872 | tf_op jit(solution)/shard_map/transpose(jvp())/scatter-add | solution.py:33
  1013.7 142.5 %all-reduce.17.cloned.1.call-done = (f32[64,128]{1,0:T(8,128)}, f32[64,64]{1,0:T(8,128)}, f32[64,128]{1,0:T(8,128)}, f32[64,64]{1,0:T(8,128)}, f32[64,64]{1,0:T(...) async-done(((f32[64,128]{1,0:T(8,128)}, f32[64,64]{1,0:T(8,128)}, f32[64,128]{1,0:T(8,128)}, f32[64,64]{1,0:T(8,128)}, f32[64,64]{1,0:T(8,128)}, ...) | async-done | bytes 164624 | tf_op jit(solution)/shard_map/psum | solution.py:208
  1156.4 3.7 scatter_fusion
  1161.2 56.1 %all-reduce.19.cloned.1.call-done = (f32[64,128]{1,0:T(8,128)}, f32[64,64]{1,0:T(8,128)}, f32[64,128]{1,0:T(8,128)}, f32[64,64]{1,0:T(8,128)}, f32[64,64]{1,0:T(...) async-done(((f32[64,128]{1,0:T(8,128)}, f32[64,64]{1,0:T(8,128)}, f32[64,128]{1,0:T(8,128)}, f32[64,64]{1,0:T(8,128)}, f32[64,64]{1,0:T(8,128)}, ...) | async-done | bytes 164624 | tf_op jit(solution)/shard_map/psum | solution.py:207
  (186 shorter events, 126.8 us)
Async XLA Ops:
  7.2 359.9 %copy-start = (f32[64,64]{1,0:T(8,128)S(1)}, f32[64,64]{1,0:T(8,128)}, u32[]{:S(2)}) copy-start(f32[64,64]{1,0:T(8,128)} %param.37) | copy-start | bytes 49156
  7.2 357.4 %all-reduce.13.cloned.1.call-start = ((), (), s32[]{:S(2)}) async-start(), calls=%async_computation | async-start | bytes 1048576 | tf_op jit(solution)/shard_map/psum | solution.py:119
  10.5 22.6 %collective-permute-start.3 = (f32[64,128]{1,0:T(8,128)S(1)}, f32[64,128]{1,0:T(8,128)S(1)}, u32[]{:S(2)}, u32[]{:S(2)}) collective-permute-start(f32[64,128]{1,0:T(8,128)S(1)} %get-tuple-element.226), channel_id=1, source_target_pairs={{1,0},{2,1},{3,2},{4,3},{5,4},{6,5},{7,6},{8,7},{9,8},{10,9},{11,1... | collective-permute-start | bytes 98312 | tf_op jit(solution)/shard_map/ppermute | solution.py:14
  11.8 21.3 %collective-permute-start.2 = (f32[64,128]{1,0:T(8,128)S(1)}, f32[64,128]{1,0:T(8,128)S(1)}, u32[]{:S(2)}, u32[]{:S(2)}) collective-permute-start(f32[64,128]{1,0:T(8,128)S(1)} %get-tuple-element.227), channel_id=1, source_target_pairs={{0,1},{1,2},{2,3},{3,4},{4,5},{5,6},{6,7},{7,8},{8,9},{9,10},{10,1... | collective-permute-start | bytes 98312 | tf_op jit(solution)/shard_map/ppermute | solution.py:14
  16.3 16.7 %collective-permute-start.1 = (f32[64,128]{1,0:T(8,128)S(1)}, f32[64,128]{1,0:T(8,128)S(1)}, u32[]{:S(2)}, u32[]{:S(2)}) collective-permute-start(f32[64,128]{1,0:T(8,128)S(1)} %get-tuple-element.228), channel_id=1, source_target_pairs={{32,0},{64,32},{96,64},{128,96},{160,128},{192,160},{224,192},{33,... | collective-permute-start | bytes 98312 | tf_op jit(solution)/shard_map/ppermute | solution.py:14
  18.3 14.7 %collective-permute-start = (f32[64,128]{1,0:T(8,128)S(1)}, f32[64,128]{1,0:T(8,128)S(1)}, u32[]{:S(2)}, u32[]{:S(2)}) collective-permute-start(f32[64,128]{1,0:T(8,128)S(1)} %get-tuple-element.229), channel_id=1, source_target_pairs={{0,32},{32,64},{64,96},{96,128},{128,160},{160,192},{192,224},{1,3... | collective-permute-start | bytes 98312 | tf_op jit(solution)/shard_map/ppermute | solution.py:14
  23.7 12.1 copy-start.23
  27.2 63.4 %copy-start.3 = (f32[64,2048]{0,1:T(8,128)}, f32[64,2048]{0,1:T(8,128)S(1)}, u32[]{:S(2)}) copy-start(f32[64,2048]{0,1:T(8,128)S(1)} %fusion.81) | copy-start | bytes 1572868
  90.6 9.8 copy-start.16
  100.4 264.2 %copy-start.21 = (f32[64,64]{1,0:T(8,128)S(1)}, f32[64,64]{1,0:T(8,128)}, u32[]{:S(2)}) copy-start(f32[64,64]{1,0:T(8,128)} %param.36) | copy-start | bytes 49156
  107.4 353.2 %copy-start.20 = (f32[64,64]{1,0:T(8,128)S(1)}, f32[64,64]{1,0:T(8,128)}, u32[]{:S(2)}) copy-start(f32[64,64]{1,0:T(8,128)} %param.38) | copy-start | bytes 49156
  108.3 750.8 %all-reduce.15.cloned.1.call-start = ((), (), s32[]{:S(2)}) async-start(), calls=%async_computation.1 | async-start | bytes 1048576 | tf_op jit(solution)/shard_map/psum | solution.py:119
  462.8 11.1 copy-start.28
  462.8 15.5 %copy-start.25 = (f32[64,64]{1,0:T(8,128)S(1)}, f32[64,64]{1,0:T(8,128)}, u32[]{:S(2)}) copy-start(f32[64,64]{1,0:T(8,128)} %param.40) | copy-start | bytes 49156
  608.4 547.8 %all-reduce.17.cloned.1.call-start = ((), (), s32[]{:S(2)}) async-start(), calls=%async_computation.2 | async-start | bytes 462848 | tf_op jit(solution)/shard_map/psum | solution.py:208
  864.3 15.3 %copy-start.30 = (f32[64,64]{1,0:T(8,128)S(1)}, f32[64,64]{1,0:T(8,128)}, u32[]{:S(2)}) copy-start(f32[64,64]{1,0:T(8,128)} %param.35) | copy-start | bytes 49156
  874.1 14.6 %copy-start.4 = (f32[64,2048]{0,1:T(8,128)S(1)}, f32[64,2048]{0,1:T(8,128)}, u32[]{:S(2)}) copy-start(f32[64,2048]{0,1:T(8,128)} %copy-done.3) | copy-start | bytes 1572868
  897.7 94.2 %copy-start.6 = (f32[64,2560]{1,0:T(8,128)S(1)}, f32[64,2560]{1,0:T(8,128)}, u32[]{:S(2)}) copy-start(f32[64,2560]{1,0:T(8,128)} %copy-done.5) | copy-start | bytes 1966084
  991.9 228.2 %copy-start.27 = (f32[64]{0:T(128)S(1)}, f32[64]{0:T(128)}, u32[]{:S(2)}) copy-start(f32[64]{0:T(128)} %get-tuple-element.239) | copy-start | bytes 772
  997.5 158.8 %collective-permute-start.4 = (f32[64,128]{1,0:T(8,128)S(1)}, f32[64,128]{1,0:T(8,128)S(1)}, u32[]{:S(2)}, u32[]{:S(2)}) collective-permute-start(f32[64,128]{1,0:T(8,128)S(1)} %get-tuple-element.222), channel_id=1, source_target_pairs={{32,0},{64,32},{96,64},{128,96},{160,128},{192,160},{224,192},{33,... | collective-permute-start | bytes 98312 | tf_op jit(solution)/shard_map/ppermute | solution.py:14
  999.4 156.8 %collective-permute-start.7 = (f32[64,128]{1,0:T(8,128)S(1)}, f32[64,128]{1,0:T(8,128)S(1)}, u32[]{:S(2)}, u32[]{:S(2)}) collective-permute-start(f32[64,128]{1,0:T(8,128)S(1)} %get-tuple-element.223), channel_id=1, source_target_pairs={{0,1},{1,2},{2,3},{3,4},{4,5},{5,6},{6,7},{7,8},{8,9},{9,10},{10,1... | collective-permute-start | bytes 98312 | tf_op jit(solution)/shard_map/ppermute | solution.py:14
  1001.3 154.9 %collective-permute-start.6 = (f32[64,128]{1,0:T(8,128)S(1)}, f32[64,128]{1,0:T(8,128)S(1)}, u32[]{:S(2)}, u32[]{:S(2)}) collective-permute-start(f32[64,128]{1,0:T(8,128)S(1)} %get-tuple-element.224), channel_id=1, source_target_pairs={{1,0},{2,1},{3,2},{4,3},{5,4},{6,5},{7,6},{8,7},{9,8},{10,9},{11,1... | collective-permute-start | bytes 98312 | tf_op jit(solution)/shard_map/ppermute | solution.py:14
  1002.6 153.6 %collective-permute-start.5 = (f32[64,128]{1,0:T(8,128)S(1)}, f32[64,128]{1,0:T(8,128)S(1)}, u32[]{:S(2)}, u32[]{:S(2)}) collective-permute-start(f32[64,128]{1,0:T(8,128)S(1)} %get-tuple-element.225), channel_id=1, source_target_pairs={{0,32},{32,64},{64,96},{96,128},{128,160},{160,192},{192,224},{1,3... | collective-permute-start | bytes 98312 | tf_op jit(solution)/shard_map/ppermute | solution.py:14
  1008.1 209.2 %all-reduce.19.cloned.1.call-start = ((), (), s32[]{:S(2)}) async-start(), calls=%async_computation.3 | async-start | bytes 462848 | tf_op jit(solution)/shard_map/psum | solution.py:207
  (19 other events, 94.2 us)
Sparse Core Ops, SparseCore 0:
  108.4 256.1 all-reduce.12
  608.5 250.5 all-reduce.14
  1008.3 147.8 all-reduce.16
  1158.9 58.3 all-reduce.18
